TPU v7x, 128 devices: a whole 4x4x4 slice. The times are simulated.
128 devices in a mesh: blk: 8 (over y, z_lo), mode: 16 (over z_hi, x, core).
Axes of the slice: x: 4, y: 4, z: 4 (z_hi: 2, z_lo: 2; z = z_hi * 2 + z_lo), core: 2. Of those that a mesh axis runs over, the one named last changes fastest.
Arguments:
- density: bfloat16 [2, 256, 2048, 256], P(None, 'mode', 'blk'), may hold values from -6 to 6
- kernel_tiles: bfloat16 [256, 16, 8, 2, 128, 128], P('mode', 'blk'), may hold values from -0.125 to 0.125
- tile_index: int32 [256, 16, 8], P('mode', 'blk'), may hold values from 0 to 1
- coupling: bfloat16 [2, 9, 256, 2048], P(None, None, 'mode', 'blk'), may hold values from -4 to 4
- spread: int32 [2048], P('blk'), may hold values from 0 to 4
- liner: int32 [2048], P('blk'), may hold values 0 or 1
Outputs:
- applied: bfloat16 [2, 256, 2048, 256], P(None, 'mode', 'blk')
Inputs may be any that keep to these rules, and one draw needn't show every extreme that they name: `tile_index`: each retained tile names one column tile of its source shard.
All inputs are finite; a program needn't handle non-finite values. No bound on the sum of `liner` on one device may be relied on, other than what follows from the above.
Results may differ from a plain program's by a relative error of at most 0.0033.
Values may be sent and summed in bfloat16 or wider, within the bound.
No kernel may reach another device: no remote copies, remote signals or barrier semaphores. Data moves between devices by JAX's collectives and lax.ppermute only.
A program may use at most 320 MiB of HBM per device.

v0:
```python
import jax
import jax.numpy as jnp
from jax import lax
from jax.sharding import PartitionSpec as P


def with_halo(block, sides, width):
    for axis, dim in sides:
        count = lax.axis_size(axis)
        forward = [(i, i + 1) for i in range(count - 1)]
        backward = [(target, source) for source, target in forward]
        low = lax.ppermute(
            lax.slice_in_dim(block, block.shape[dim] - width, None, axis=dim), axis, forward
        )
        high = lax.ppermute(lax.slice_in_dim(block, 0, width, axis=dim), axis, backward)
        block = jnp.concatenate([low, block, high], axis=dim)
    return block


def tile_product(left, right):
    return jnp.einsum("mtqk,mtkr->mtqr", left, right, preferred_element_type=jnp.float32)


def couple_modes(padded, weights, mode_count):
    band_count = weights.shape[1]
    real_part = jnp.zeros((mode_count,) + padded.shape[2:], jnp.float32)
    imag_part = jnp.zeros((mode_count,) + padded.shape[2:], jnp.float32)
    for offset in range(band_count):
        shifted = padded[:, offset : offset + mode_count].astype(jnp.float32)
        weight_now = weights[:, offset].astype(jnp.float32)[..., None]
        real_part = real_part + weight_now[0] * shifted[0] - weight_now[1] * shifted[1]
        imag_part = imag_part + weight_now[0] * shifted[1] + weight_now[1] * shifted[0]
    return jnp.stack([real_part, imag_part]).astype(jnp.bfloat16)


def shards(density, kernel_tiles, tile_index, coupling, spread, liner):
    mode_count = density.shape[1]
    point_count = density.shape[2]
    rhs_count = density.shape[3]
    tile_size = kernel_tiles.shape[-1]
    row_tiles = kernel_tiles.shape[1]
    per_shard = point_count // tile_size
    band_count = coupling.shape[1]
    reach = band_count // 2
    column_ids = jnp.arange(per_shard, dtype=jnp.int32)
    initial = jnp.zeros((2, mode_count, row_tiles, tile_size, rhs_count), jnp.float32)
    gathered = lax.all_gather(density, "blk", axis=2, tiled=True)
    shard_count = gathered.shape[2] // point_count

    def one_shard(position, running):
        shard_block = lax.dynamic_slice_in_dim(gathered, position * point_count, point_count, 2)
        shard_block = shard_block.reshape(2, mode_count, per_shard, tile_size, rhs_count)
        chosen_tiles = lax.dynamic_index_in_dim(tile_index, position, 2, keepdims=False)
        one_hot = (chosen_tiles[:, :, None] == column_ids).astype(jnp.bfloat16)
        picked_tiles = jnp.einsum(
            "mts,cmsqr->cmtqr", one_hot, shard_block, preferred_element_type=jnp.float32
        ).astype(jnp.bfloat16)
        kernel_block = lax.dynamic_index_in_dim(kernel_tiles, position, 2, keepdims=False)
        real_part = tile_product(kernel_block[:, :, 0], picked_tiles[0]) - tile_product(
            kernel_block[:, :, 1], picked_tiles[1]
        )
        imag_part = tile_product(kernel_block[:, :, 0], picked_tiles[1]) + tile_product(
            kernel_block[:, :, 1], picked_tiles[0]
        )
        return running + jnp.stack([real_part, imag_part])

    near = lax.fori_loop(0, shard_count, one_shard, initial)
    near = near.reshape(2, mode_count, point_count, rhs_count)
    offsets = jnp.abs(jnp.arange(band_count, dtype=jnp.int32) - reach)
    within = (offsets[:, None] <= spread[None, :]) & (liner[None, :] == 1)
    weights = coupling * within[None, :, None, :].astype(jnp.bfloat16)
    extended = with_halo(density, (("mode", 1),), reach)
    coupled = couple_modes(extended, weights, mode_count)
    total = 0.5 * density.astype(jnp.float32) + near + coupled.astype(jnp.float32)
    return total.astype(jnp.bfloat16)


def solution(mesh):
    return jax.shard_map(
        shards,
        mesh=mesh,
        in_specs=(
            P(None, "mode", "blk", None),
            P("mode", "blk", None, None, None, None),
            P("mode", "blk", None),
            P(None, None, "mode", "blk"),
            P("blk"),
            P("blk"),
        ),
        out_specs=P(None, "mode", "blk", None),
        check_vma=False,
    )
```

profile of v0, /device:TPU:1, one launch (start us, length us, event | category | flops | bytes accessed | tf_op | source)
XLA Modules:
  0.0 1023.9 jit_solution(228144644666771216)
XLA Ops:
  17.0 9.9 collective-permute-done
  26.9 7.9 constant_dynamic-update-slice_fusion
  37.2 11.7 %slice_convert_fusion.3 = (f32[2,16,256,256]{3,2,1,0:T(8,128)}, f32[2,16,256,256]{3,2,1,0:T(8,128)}, f32[2,16,256,256]{3,2,1,0:T(8,128)}, f32[2,16,256,256]{3,2,1,0:T(8,128)}) fusion(bf16[2,20,256,256]{3,2,1,0:T(8,128)(2,1)S(1)} %constant_dynamic-update-slice_fusion.2), kind=kLoop, calls=%fused_computation.30 | loop fusion | flops 8388608 | bytes 50331648 | tf_op jit(solution)/shard_map/convert_element_type | solution.py:29
  48.9 15.3 %slice_convert_fusion.7 = (f32[2,16,256,256]{3,2,1,0:T(8,128)}, f32[2,16,256,256]{3,2,1,0:T(8,128)}, f32[2,16,256,256]{3,2,1,0:T(8,128)}, f32[2,16,256,256]{3,2,1,0:T(8,128)}) fusion(bf16[2,20,256,256]{3,2,1,0:T(8,128)(2,1)} %copy-done), kind=kLoop, calls=%fused_computation.34 | loop fusion | flops 8388608 | bytes 50331648 | tf_op jit(solution)/shard_map/convert_element_type | solution.py:29
  64.2 24.6 %subtract_convert_fusion = bf16[1,16,256,256]{3,2,1,0:T(8,128)(2,1)} fusion(f32[2,16,256,256]{3,2,1,0:T(8,128)} %get-tuple-element.162, f32[2,16,256,256]{3,2,1,0:T(8,128)} %get-tuple-element.163, f32[2,16,256,256]{3,2,1,0:T(8,128)} %get-tuple-element.164, f32[2,16,256,256]{3,2,1,0:T(8,128)} %get-tuple-element.161, ...), kind=kLoop, calls=%fused_computation.36 | loop fusion | flops 37748736 | bytes 77889536 | tf_op jit(solution)/shard_map/convert
  88.8 25.0 %add_convert_fusion = bf16[1,16,256,256]{3,2,1,0:T(8,128)(2,1)} fusion(f32[2,16,256,256]{3,2,1,0:T(8,128)} %get-tuple-element.162, f32[2,16,256,256]{3,2,1,0:T(8,128)} %get-tuple-element.163, f32[2,16,256,256]{3,2,1,0:T(8,128)} %get-tuple-element.164, f32[2,16,256,256]{3,2,1,0:T(8,128)} %get-tuple-element.161, f32[2,16,256,256]{3,2,1,0:T(8,128)} %get-tuple-element.166, ...), kind=kLoop, calls=%fused_computation.35 | loop fusion | flops 37748736 | bytes 77889536 | tf_op jit(solution)/shard_map/convert.1
  113.8 548.6 %all-gather.2.cloned.1.call-done = bf16[2,16,2048,256]{3,2,1,0:T(8,128)(2,1)} async-done(((bf16[2,16,256,256]{3,2,1,0:T(8,128)(2,1)}), bf16[2,16,2048,256]{3,2,1,0:T(8,128)(2,1)}) %all-gather.2.cloned.1.call-update) | async-done | bytes 33554448 | tf_op jit(solution)/shard_map/all_gather | solution.py:47
  662.4 346.8 %while.14 = (s32[]{:T(128)}, f32[2,16,2,128,256]{4,3,2,1,0:T(8,128)}, bf16[16,2,8,2,128,128]{5,4,3,2,1,0:T(8,128)(2,1)}, bf16[2,16,2048,256]{3,2,1,0:T(8,128)(2,...) while((s32[]{:T(128)}, f32[2,16,2,128,256]{4,3,2,1,0:T(8,128)}, ...), condition=%wide.region_1.2_spmd.clone, body=%wide.region_0.1_spmd.clone.sunk | while | flops 1092616192 | bytes 92275992 | solution.py:67
  662.4 4.8 constant_dynamic-slice_fusion.8
  667.9 16.7 %fusion.28 = bf16[2,16,2,128,256]{4,2,3,0,1:T(2,128)(2,1)S(1)} fusion(bf16[2,16,2,128,256]{4,3,2,1,0:T(8,128)(2,1)} %bitcast.95, s32[16,2]{1,0:T(8,128)S(1)} %copy.49), kind=kOutput, calls=%fused_computation.3.clone.1 | convolution fusion | flops 10485824 | bytes 8388736 | tf_op jit(solution)/shard_map/while/body/eval_jaxpr/mts,cmsqr->cmtqr/dot_general | solution.py:55
  696.2 6.3 maximum_add_fusion.2
  702.5 4.6 constant_dynamic-slice_fusion.8
  707.9 16.7 %fusion.28 = bf16[2,16,2,128,256]{4,2,3,0,1:T(2,128)(2,1)S(1)} fusion(bf16[2,16,2,128,256]{4,3,2,1,0:T(8,128)(2,1)} %bitcast.95, s32[16,2]{1,0:T(8,128)S(1)} %copy.49), kind=kOutput, calls=%fused_computation.3.clone.1 | convolution fusion | flops 10485824 | bytes 8388736 | tf_op jit(solution)/shard_map/while/body/eval_jaxpr/mts,cmsqr->cmtqr/dot_general | solution.py:55
  736.2 10.1 maximum_add_fusion.2
  746.3 4.6 constant_dynamic-slice_fusion.8
  751.7 16.7 %fusion.28 = bf16[2,16,2,128,256]{4,2,3,0,1:T(2,128)(2,1)S(1)} fusion(bf16[2,16,2,128,256]{4,3,2,1,0:T(8,128)(2,1)} %bitcast.95, s32[16,2]{1,0:T(8,128)S(1)} %copy.49), kind=kOutput, calls=%fused_computation.3.clone.1 | convolution fusion | flops 10485824 | bytes 8388736 | tf_op jit(solution)/shard_map/while/body/eval_jaxpr/mts,cmsqr->cmtqr/dot_general | solution.py:55
  780.1 10.1 maximum_add_fusion.2
  790.1 4.6 constant_dynamic-slice_fusion.8
  795.6 16.7 %fusion.28 = bf16[2,16,2,128,256]{4,2,3,0,1:T(2,128)(2,1)S(1)} fusion(bf16[2,16,2,128,256]{4,3,2,1,0:T(8,128)(2,1)} %bitcast.95, s32[16,2]{1,0:T(8,128)S(1)} %copy.49), kind=kOutput, calls=%fused_computation.3.clone.1 | convolution fusion | flops 10485824 | bytes 8388736 | tf_op jit(solution)/shard_map/while/body/eval_jaxpr/mts,cmsqr->cmtqr/dot_general | solution.py:55
  823.9 10.1 maximum_add_fusion.2
  833.9 4.6 constant_dynamic-slice_fusion.8
  839.4 16.7 %fusion.28 = bf16[2,16,2,128,256]{4,2,3,0,1:T(2,128)(2,1)S(1)} fusion(bf16[2,16,2,128,256]{4,3,2,1,0:T(8,128)(2,1)} %bitcast.95, s32[16,2]{1,0:T(8,128)S(1)} %copy.49), kind=kOutput, calls=%fused_computation.3.clone.1 | convolution fusion | flops 10485824 | bytes 8388736 | tf_op jit(solution)/shard_map/while/body/eval_jaxpr/mts,cmsqr->cmtqr/dot_general | solution.py:55
  867.7 10.1 maximum_add_fusion.2
  883.2 16.7 %fusion.28 = bf16[2,16,2,128,256]{4,2,3,0,1:T(2,128)(2,1)S(1)} fusion(bf16[2,16,2,128,256]{4,3,2,1,0:T(8,128)(2,1)} %bitcast.95, s32[16,2]{1,0:T(8,128)S(1)} %copy.49), kind=kOutput, calls=%fused_computation.3.clone.1 | convolution fusion | flops 10485824 | bytes 8388736 | tf_op jit(solution)/shard_map/while/body/eval_jaxpr/mts,cmsqr->cmtqr/dot_general | solution.py:55
  911.5 10.1 maximum_add_fusion.2
  921.6 4.6 constant_dynamic-slice_fusion.8
  927.0 16.7 %fusion.28 = bf16[2,16,2,128,256]{4,2,3,0,1:T(2,128)(2,1)S(1)} fusion(bf16[2,16,2,128,256]{4,3,2,1,0:T(8,128)(2,1)} %bitcast.95, s32[16,2]{1,0:T(8,128)S(1)} %copy.49), kind=kOutput, calls=%fused_computation.3.clone.1 | convolution fusion | flops 10485824 | bytes 8388736 | tf_op jit(solution)/shard_map/while/body/eval_jaxpr/mts,cmsqr->cmtqr/dot_general | solution.py:55
  955.3 10.1 maximum_add_fusion.2
  965.4 4.6 constant_dynamic-slice_fusion.8
  970.8 16.7 %fusion.28 = bf16[2,16,2,128,256]{4,2,3,0,1:T(2,128)(2,1)S(1)} fusion(bf16[2,16,2,128,256]{4,3,2,1,0:T(8,128)(2,1)} %bitcast.95, s32[16,2]{1,0:T(8,128)S(1)} %copy.49), kind=kOutput, calls=%fused_computation.3.clone.1 | convolution fusion | flops 10485824 | bytes 8388736 | tf_op jit(solution)/shard_map/while/body/eval_jaxpr/mts,cmsqr->cmtqr/dot_general | solution.py:55
  999.1 10.1 maximum_add_fusion.2
  1009.2 7.8 fusion.13
  (94 shorter events, 116.1 us)
Async XLA Ops:
  6.5 10.2 %copy-start.4 = (s32[256]{0:T(256)S(1)}, s32[256]{0:T(256)}, u32[]{:S(2)}) copy-start(s32[256]{0:T(256)} %param.13) | copy-start | bytes 3076
  6.5 10.3 %copy-start.3 = (s32[256]{0:T(256)S(1)}, s32[256]{0:T(256)}, u32[]{:S(2)}) copy-start(s32[256]{0:T(256)} %param.12) | copy-start | bytes 3076
  6.5 10.4 %copy-start.2 = (bf16[2,9,16,256]{3,2,1,0:T(8,128)(2,1)S(1)}, bf16[2,9,16,256]{3,2,1,0:T(8,128)(2,1)}, u32[]{:S(2)}) copy-start(bf16[2,9,16,256]{3,2,1,0:T(8,128)(2,1)} %param.11) | copy-start | bytes 442372
  6.5 655.8 %all-gather.2.cloned.1.call-start = ((), (), s32[]{:S(2)}) async-start(), calls=%async_computation | async-start | bytes 37748736 | tf_op jit(solution)/shard_map/all_gather | solution.py:47
  10.3 16.5 %collective-permute-start = (bf16[2,4,256,256]{3,2,1,0:T(8,128)(2,1)}, bf16[2,4,256,256]{3,2,1,0:T(8,128)(2,1)S(1)}, u32[]{:S(2)}, u32[]{:S(2)}) collective-permute-start(bf16[2,4,256,256]{3,2,1,0:T(8,128)(2,1)} %get-tuple-element.168), channel_id=1, source_target_pairs={{0,1},{1,2},{2,3},{3,4},{4,5},{5,6},{6,7},{7,8},{8,9},{9,10},{10,1... | collective-permute-start | bytes 3145736 | tf_op jit(solution)/shard_map/ppermute | solution.py:12
  14.8 20.1 %collective-permute-start.1 = (bf16[2,4,256,256]{3,2,1,0:T(8,128)(2,1)}, bf16[2,4,256,256]{3,2,1,0:T(8,128)(2,1)S(1)}, u32[]{:S(2)}, u32[]{:S(2)}) collective-permute-start(bf16[2,4,256,256]{3,2,1,0:T(8,128)(2,1)} %get-tuple-element.169), channel_id=1, source_target_pairs={{1,0},{2,1},{3,2},{4,3},{5,4},{6,5},{7,6},{8,7},{9,8},{10,9},{11,1... | collective-permute-start | bytes 3145736 | tf_op jit(solution)/shard_map/ppermute | solution.py:15
  34.9 2.3 copy-start
  662.4 346.8 %copy-start.1 = (bf16[1,16,256,256]{3,2,1,0:T(8,128)(2,1)S(1)}, bf16[1,16,256,256]{3,2,1,0:T(8,128)(2,1)}, u32[]{:S(2)}) copy-start(bf16[1,16,256,256]{3,2,1,0:T(8,128)(2,1)} %subtract_convert_fusion) | copy-start | bytes 6291460
Sparse Core Ops, SparseCore 0:
  9.0 653.3 all-gather.1
where the time goes:
time: 1020 us
  waiting for transfers between devices  559 us (55%)
  matrix products  188 us (18%)
  other arithmetic  169 us (17%)
  local copies, waits for them, and re-layouts  87.5 us (9%)
  between operations  13.5 us (1%)
    all_gather x1, waiting for transfers between devices, shards(): gathered = lax.all_gather(density, 'blk', axis=2, tiled=True)  549 us
    dot_general x8, matrix products, one_shard(): jnp.einsum('mts,cmsqr->cmtqr', one_hot, shard_block, preferred_element_ty...  134 us
    add x8, other arithmetic, one_shard(): return running + jnp.stack([real_part, imag_part])  76.8 us
    dot_general x32, matrix products, tile_product(): jnp.einsum('mtqk,mtkr->mtqr', left, right, preferred_element_type=jnp.flo...  54 us
    another operation x2, other arithmetic  49.6 us
    dynamic_slice x8, local copies, waits for them, and re-layouts, one_shard(): lax.dynamic_slice_in_dim(gathered, position * point_count, point_count, 2)  37.3 us
    convert_element_type x2, other arithmetic, couple_modes(): shifted = padded[:, offset:offset + mode_count].astype(jnp.float32)  27 us
    squeeze x8, local copies, waits for them, and re-layouts, one_shard(): picked_tiles[0]  23.6 us
  transfers between devices with their start and end apart: 3, of which 2 were waited for; matrix products, arithmetic and copies ran while one was open for 9% of the time, Pallas kernels for 0%

commit v1 on v0

v1 whole, which is shorter than its diff:
```python
import functools

import jax
import jax.numpy as jnp
from jax import lax
from jax.experimental import pallas as pl
from jax.experimental.pallas import tpu as pltpu
from jax.sharding import PartitionSpec as P


TILE = 128
PARTS = ((5, 0, 1, 2, (2, 2, 1)), (5, 1, 2, 0, (2, 2, 1)), (6, 2, 0, 1, (2, 2, 2)))


def blk_of(node):
    gray = node & 3
    return (gray ^ (gray >> 1)) * 2 + (node >> 2)


def node_of(blk):
    y = blk // 2
    return (y ^ (y >> 1)) | ((blk % 2) << 2)


def swap(block, direction):
    pairs = [(blk_of(node), blk_of(node ^ (1 << direction))) for node in range(8)]
    return lax.ppermute(block, "blk", pairs)


def near_rows(index_ref, shard_ref, first, row, kernels, density_refs):
    left, right = [], []
    for slot, density_ref in enumerate(density_refs):
        tile = index_ref[first + row * 8 + shard_ref[slot]]
        at = pl.ds(pl.multiple_of(tile * TILE, TILE), TILE)
        right.append(jnp.concatenate([density_ref[0, 0, at, :], density_ref[1, 0, at, :]], axis=1))
        left.append(kernels(slot, row))
    product = jnp.dot(
        jnp.concatenate(left, axis=1),
        jnp.concatenate(right, axis=0),
        preferred_element_type=jnp.float32,
    )
    width = product.shape[1] // 2
    real_part = product[:TILE, :width] - product[TILE:, width:]
    imag_part = product[:TILE, width:] + product[TILE:, :width]
    return real_part, imag_part


class Steps:
    def __init__(self, starts, offsets, sizes):
        self.starts, self.offsets, self.sizes = starts, offsets, sizes
        self.bounds = [sum(sizes[:at]) for at in range(len(sizes) + 1)]

    def part(self, step):
        return sum((step >= bound).astype(jnp.int32) for bound in self.bounds[1:-1])

    def mode(self, step):
        found = step - self.bounds[0] + self.starts[0] + self.offsets[0]
        for at in range(1, len(self.sizes)):
            here = step - self.bounds[at] + self.starts[at] + self.offsets[at]
            found = jnp.where(step >= self.bounds[at], here, found)
        return found

    def within(self, at, step):
        return jnp.clip(step - self.bounds[at], 0, self.sizes[at] - 1)

    def whole_spec(self, points, rhs):
        return pl.BlockSpec((2, 1, points, rhs), lambda i, *_: (0, self.mode(i), 0, 0))

    def piece_spec(self, at, points, rhs, offset=0):
        return pl.BlockSpec((2, 1, points, rhs), lambda i, *_: (0, offset + self.within(at, i), 0, 0))


def partial_kernel(steps, index0, index1, index2, shard_ref, *refs):
    index_refs, kernel_refs, density_refs, out_refs = (index0, index1, index2), refs[:3], refs[3:15], refs[15:]
    step = pl.program_id(0)
    part = steps.part(step)
    first = steps.mode(step) * 16
    for at in range(3):

        @pl.when(part == at)
        def _(at=at):
            for row in range(2):
                sums = near_rows(
                    index_refs[at], shard_ref.at[pl.ds(4 * at, 4)], first, row,
                    lambda slot, row: kernel_refs[at][0, row, slot].reshape(2 * TILE, TILE),
                    density_refs[4 * at : 4 * at + 4],
                )
                for c in range(2):
                    out_refs[at][c, 0, pl.ds(row * TILE, TILE), :] = sums[c].astype(jnp.bfloat16)


def partial_near(steps, indexes, shard_ids, kernels, densities):
    rows, slots = kernels[0].shape[1:3]
    points, rhs = densities[0].shape[2:]
    count = sum(steps.sizes)
    return pl.pallas_call(
        functools.partial(partial_kernel, steps),
        grid_spec=pltpu.PrefetchScalarGridSpec(
            num_scalar_prefetch=4,
            grid=(count,),
            in_specs=[
                pl.BlockSpec((1, rows, slots, 2, TILE, TILE), lambda i, *_, at=at: (steps.within(at, i), 0, 0, 0, 0, 0))
                for at in range(3)
            ]
            + [steps.piece_spec(at, points, rhs, steps.offsets[at]) for at in range(3) for _ in range(4)],
            out_specs=[steps.piece_spec(at, points, rhs) for at in range(3)],
        ),
        out_shape=[jax.ShapeDtypeStruct((2, size, points, rhs), jnp.bfloat16) for size in steps.sizes],
        cost_estimate=pl.CostEstimate(flops=count * 540_000_000, bytes_accessed=count * 1_900_000, transcendentals=0),
        name="partial_near",
    )(*indexes, shard_ids, *kernels, *densities)


def own_kernel(steps, index_ref, shard_ref, *refs):
    kernel_refs, density_refs, own_ref, coupled_ref, out_ref = refs[:4], refs[4:16], refs[16], refs[17], refs[18]
    step = pl.program_id(0)
    part = steps.part(step)
    first = steps.mode(step) * 16
    for at in range(3):

        @pl.when(part == at)
        def _(at=at):
            for row in range(2):
                sums = near_rows(
                    index_ref, shard_ref.at[pl.ds(4 * at, 4)], first, row,
                    lambda slot, row: kernel_refs[slot][0, row, 0].reshape(2 * TILE, TILE),
                    density_refs[4 * at : 4 * at + 4],
                )
                rows = pl.ds(row * TILE, TILE)
                for c in range(2):
                    total = 0.5 * own_ref[c, 0, rows, :].astype(jnp.float32) + sums[c]
                    out_ref[c, 0, rows, :] = total + coupled_ref[c, 0, rows, :].astype(jnp.float32)


def own_near(steps, index, shard_ids, kernel_tiles, densities, density, coupled):
    rows = kernel_tiles.shape[1]
    points, rhs = density.shape[2:]
    count = sum(steps.sizes)

    def kernel_spec(slot):
        return pl.BlockSpec(
            (1, rows, 1, 2, TILE, TILE),
            lambda i, index_ref, shard_ref: (steps.mode(i), 0, shard_ref[4 * steps.part(i) + slot], 0, 0, 0),
        )

    return pl.pallas_call(
        functools.partial(own_kernel, steps),
        grid_spec=pltpu.PrefetchScalarGridSpec(
            num_scalar_prefetch=2,
            grid=(count,),
            in_specs=[kernel_spec(slot) for slot in range(4)]
            + [steps.piece_spec(at, points, rhs, steps.offsets[at]) for at in range(3) for _ in range(4)]
            + [steps.whole_spec(points, rhs)] * 2,
            out_specs=steps.whole_spec(points, rhs),
        ),
        out_shape=jax.ShapeDtypeStruct(density.shape, jnp.float32),
        cost_estimate=pl.CostEstimate(flops=count * 540_000_000, bytes_accessed=count * 2_600_000, transcendentals=0),
        name="own_near",
    )(index, shard_ids, *([kernel_tiles] * 4), *densities, density, coupled)


def final_kernel(steps, base_ref, o0, o1, o2, *refs):
    out_ref = refs[-1]
    part = steps.part(pl.program_id(0))
    for at, other_ref in enumerate((o0, o1, o2)):

        @pl.when(part == at)
        def _(other_ref=other_ref):
            out_ref[...] = (base_ref[...] + other_ref[...].astype(jnp.float32)).astype(out_ref.dtype)


def final_sum(steps, base, others, running):
    points, rhs = base.shape[2:]
    count = sum(steps.sizes)
    ins = [base, *others] + ([] if running is None else [running])
    return pl.pallas_call(
        functools.partial(final_kernel, steps),
        grid=(count,),
        in_specs=[steps.whole_spec(points, rhs)]
        + [steps.piece_spec(at, points, rhs) for at in range(3)]
        + ([] if running is None else [pl.BlockSpec(memory_space=pl.ANY)]),
        out_specs=steps.whole_spec(points, rhs),
        out_shape=jax.ShapeDtypeStruct(base.shape, jnp.bfloat16),
        input_output_aliases={} if running is None else {4: 0},
        cost_estimate=pl.CostEstimate(flops=count * 262144, bytes_accessed=count * 1_050_000, transcendentals=0),
        name="final_sum",
    )(*ins)


def pack_kernel(chunk_sizes, shard_ref, k0, k1, k2, k3, *out_refs):
    step = pl.program_id(0)
    bound = 0
    for size, out_ref in zip(chunk_sizes, out_refs, strict=True):

        @pl.when((step >= bound) & (step < bound + size))
        def _(out_ref=out_ref):
            for slot, kernel_ref in enumerate((k0, k1, k2, k3)):
                out_ref[:, :, slot] = kernel_ref[:, :, 0]

        bound += size


def pack(steps, chunk_sizes, shard_ids, kernel_tiles):
    rows = kernel_tiles.shape[1]
    count = sum(steps.sizes)

    def kernel_spec(slot):
        return pl.BlockSpec(
            (1, rows, 1, 2, TILE, TILE),
            lambda i, shard_ref: (steps.mode(i), 0, shard_ref[4 * steps.part(i) + slot], 0, 0, 0),
        )

    def out_spec(bound, size):
        return pl.BlockSpec(
            (1, rows, 4, 2, TILE, TILE), lambda i, *_: (jnp.clip(i - bound, 0, size - 1), 0, 0, 0, 0, 0)
        )

    return pl.pallas_call(
        functools.partial(pack_kernel, chunk_sizes),
        grid_spec=pltpu.PrefetchScalarGridSpec(
            num_scalar_prefetch=1,
            grid=(count,),
            in_specs=[kernel_spec(slot) for slot in range(4)],
            out_specs=[out_spec(sum(chunk_sizes[:at]), size) for at, size in enumerate(chunk_sizes)],
        ),
        out_shape=[jax.ShapeDtypeStruct((size, rows, 4, 2, TILE, TILE), jnp.bfloat16) for size in chunk_sizes],
        cost_estimate=pl.CostEstimate(flops=0, bytes_accessed=count * 1_050_000, transcendentals=0),
        name="pack",
    )(shard_ids, *([kernel_tiles] * 4))


def couple_kernel(band, weight_ref, low_ref, own_ref, high_ref, out_ref):
    reach = band // 2
    modes = own_ref.shape[1]

    def window(c, mode):
        if mode < reach:
            return low_ref[c, mode].astype(jnp.float32)
        if mode < reach + modes:
            return own_ref[c, mode - reach].astype(jnp.float32)
        return high_ref[c, mode - reach - modes].astype(jnp.float32)

    shape = own_ref.shape[2:]
    for mode in range(modes):
        real_part = imag_part = None
        for offset in range(band):
            at = offset * modes + mode
            wr = jnp.broadcast_to(weight_ref[:, at : at + 1], shape)
            at += band * modes
            wi = jnp.broadcast_to(weight_ref[:, at : at + 1], shape)
            sr, si = window(0, mode + offset), window(1, mode + offset)
            real_now, imag_now = wr * sr - wi * si, wr * si + wi * sr
            real_part = real_now if real_part is None else real_part + real_now
            imag_part = imag_now if imag_part is None else imag_part + imag_now
        out_ref[0, mode] = real_part.astype(out_ref.dtype)
        out_ref[1, mode] = imag_part.astype(out_ref.dtype)


def couple(density, low, high, weights, rows=16):
    _, modes, points, rhs = density.shape
    band = weights.shape[1]
    reach = band // 2
    by_point = jnp.transpose(weights.astype(jnp.float32).reshape(2 * band * modes, points))

    def spec(count):
        return pl.BlockSpec((2, count, rows, rhs), lambda i: (0, 0, i, 0))

    return pl.pallas_call(
        functools.partial(couple_kernel, band),
        grid=(points // rows,),
        in_specs=[pl.BlockSpec((rows, by_point.shape[1]), lambda i: (i, 0)), spec(reach), spec(modes), spec(reach)],
        out_specs=spec(modes),
        out_shape=jax.ShapeDtypeStruct(density.shape, jnp.bfloat16),
        cost_estimate=pl.CostEstimate(flops=20_000_000_000, bytes_accessed=10_000_000, transcendentals=0),
        name="couple",
    )(by_point, low, density, high)


def apply(density, kernel_tiles, tile_index, coupling, spread, liner):
    band_count = coupling.shape[1]
    reach = band_count // 2
    mode_count = density.shape[1]
    node = node_of(lax.axis_index("blk"))
    starts = [sum(part[0] for part in PARTS[:at]) for at in range(3)]
    all_steps = Steps(starts, [0] * 3, [part[0] for part in PARTS])
    chunk_steps = [
        Steps(starts, [sum(part[4][:chunk]) for part in PARTS], [part[4][chunk] for part in PARTS]) for chunk in range(3)
    ]
    masks = [[0, 1 << one, 1 << two, (1 << one) | (1 << two)] for _, one, two, _, _ in PARTS]
    held = jnp.stack([blk_of(node ^ mask) for part in masks for mask in part])
    theirs = jnp.stack(
        [blk_of(node ^ mask ^ (1 << part[3])) for part, some in zip(PARTS, masks, strict=True) for mask in some]
    )

    own = [lax.slice_in_dim(density, start, start + part[0], axis=1) for start, part in zip(starts, PARTS, strict=True)]
    from_one, from_two, from_both, indexes = [], [], [], []
    for at, part in enumerate(PARTS):
        from_one.append(swap(own[at], part[1]))
    for at, part in enumerate(PARTS):
        from_two.append(swap(own[at], part[2]))
    devices = lax.axis_size("mode")
    forward = [(i, i + 1) for i in range(devices - 1)]
    backward = [(target, source) for source, target in forward]
    low = lax.ppermute(lax.slice_in_dim(density, mode_count - reach, None, axis=1), "mode", forward)
    high = lax.ppermute(lax.slice_in_dim(density, 0, reach, axis=1), "mode", backward)
    index = tile_index.reshape(-1)
    for part in PARTS:
        indexes.append(swap(index, part[3]))
    for at, part in enumerate(PARTS):
        from_both.append(swap(from_one[at], part[2]))
    densities = [ref for at in range(3) for ref in (own[at], from_one[at], from_two[at], from_both[at])]

    leaving = pack(all_steps, [size for part in PARTS for size in part[4]], theirs, kernel_tiles)
    kernels = {}
    for chunk in range(3):
        for at, part in enumerate(PARTS):
            kernels[chunk, at] = swap(leaving[3 * at + chunk], part[3])

    offsets = jnp.abs(jnp.arange(band_count, dtype=jnp.int32) - reach)
    within = (offsets[:, None] <= spread[None, :]) & (liner[None, :] == 1)
    weights = coupling * within[None, :, None, :].astype(jnp.bfloat16)
    coupled = couple(density, low, high, weights)
    base = own_near(all_steps, index, held, kernel_tiles, densities, density, coupled)

    others = {}
    for chunk in range(3):
        sums = partial_near(
            chunk_steps[chunk], indexes, held, [kernels[chunk, at] for at in range(3)], densities
        )
        for at, part in enumerate(PARTS):
            others[chunk, at] = swap(sums[at], part[3])
    running = None
    for chunk in range(3):
        running = final_sum(chunk_steps[chunk], base, [others[chunk, at] for at in range(3)], running)
    return running


def solution(mesh):
    return jax.shard_map(
        apply,
        mesh=mesh,
        in_specs=(
            P(None, "mode", "blk", None),
            P("mode", "blk", None, None, None, None),
            P("mode", "blk", None),
            P(None, None, "mode", "blk"),
            P("blk"),
            P("blk"),
        ),
        out_specs=P(None, "mode", "blk", None),
        check_vma=False,
    )
```

time: 1020 us -> 284 us (0.28)
  the two profiles are of different devices: /device:TPU:1 before, /device:TPU:0 now
where the time goes in v1:
time: 284 us; the launch traced here: 282 us
  waiting for transfers between devices  130 us (46%)
  Pallas kernels  92.9 us (33%)
  starting transfers between devices  44.9 us (16%)
  local copies, waits for them, and re-layouts  13.5 us (5%)
    ppermute x30, waiting for transfers between devices, swap(): return lax.ppermute(block, 'blk', pairs)  130 us
    ppermute x30, starting transfers between devices, swap(): return lax.ppermute(block, 'blk', pairs)  39.6 us
    pallas_call x3, Pallas kernels, partial_near(): pl.pallas_call(functools.partial(partial_kernel, steps), grid_spec=pltpu....  24.6 us
    pallas_call x1, Pallas kernels, own_near(): pl.pallas_call(functools.partial(own_kernel, steps), grid_spec=pltpu.Pref...  21.4 us
    pallas_call x1, Pallas kernels, couple(): pl.pallas_call(functools.partial(couple_kernel, band), grid=(points // ro...  18.3 us
    pallas_call x3, Pallas kernels, final_sum(): pl.pallas_call(functools.partial(final_kernel, steps), grid=(count,), in_...  14.4 us
    pallas_call x1, Pallas kernels, pack(): pl.pallas_call(functools.partial(pack_kernel, chunk_sizes), grid_spec=plt...  14.1 us
  transfers between devices with their start and end apart: 32, of which 9 were waited for; matrix products, arithmetic and copies ran while one was open for 3% of the time, Pallas kernels for 27%

profile of v1, /device:TPU:0, one launch (start us, length us, event | category | flops | bytes accessed | tf_op | source)
XLA Modules:
  0.0 281.8 jit_solution(10851912648101064616)
XLA Ops:
  0.6 14.1 %pack.1 = (bf16[2,2,4,2,128,128]{5,4,3,2,1,0:T(8,128)(2,1)}, bf16[2,2,4,2,128,128]{5,4,3,2,1,0:T(8,128)(2,1)}, bf16[1,2,4,2,128,128]{5,4,3,2,1,0:T(8,128)(2,1)},...) custom-call(s32[12]{0:T(128)} %stack.79.shard_ref, ...), custom_call_target="tpu_custom_call" | custom-call | bytes 16800000 | tf_op jit(solution)/shard_map/pack/pallas_call | solution.py:218
  14.7 2.1 collective-permute-start.20
  18.4 2.2 collective-permute-start.22
  22.0 22.3 %collective-permute-done.13.index2 = s32[256]{0:T(256)S(1)} collective-permute-done((s32[256]{0:T(256)S(1)}, s32[256]{0:T(256)S(1)}, u32[]{:S(2)}, u32[]{:S(2)}) %collective-permute-start.13) | collective-permute-done | bytes 1056 | tf_op jit(solution)/shard_map/ppermute | solution.py:27
  44.3 3.6 %collective-permute-done.12.index1 = s32[256]{0:T(256)S(1)} collective-permute-done((s32[256]{0:T(256)S(1)}, s32[256]{0:T(256)S(1)}, u32[]{:S(2)}, u32[]{:S(2)}) %collective-permute-start.12) | collective-permute-done | bytes 1056 | tf_op jit(solution)/shard_map/ppermute | solution.py:27
  48.2 3.0 %fusion.1 = (bf16[2,5,256,256]{3,2,1,0:T(8,128)(2,1)S(1)}, bf16[2,5,256,256]{3,2,1,0:T(8,128)(2,1)}) fusion(bf16[2,16,256,256]{3,2,1,0:T(8,128)(2,1)} %refs_16_.1), kind=kLoop, calls=%fused_computation.6 | loop fusion | bytes 5242880 | tf_op jit(solution)/shard_map/slice | solution.py:295
  51.2 11.6 %collective-permute-done.11.index0 = s32[256]{0:T(256)S(1)} collective-permute-done((s32[256]{0:T(256)S(1)}, s32[256]{0:T(256)S(1)}, u32[]{:S(2)}, u32[]{:S(2)}) %collective-permute-start.11) | collective-permute-done | bytes 1056 | tf_op jit(solution)/shard_map/ppermute | solution.py:27
  62.8 1.8 collective-permute-start.4
  68.1 2.2 collective-permute-start.3
  71.0 21.6 %collective-permute-done.27.refs_1_ = bf16[2,2,4,2,128,128]{5,4,3,2,1,0:T(8,128)(2,1)S(1)} collective-permute-done((bf16[2,2,4,2,128,128]{5,4,3,2,1,0:T(8,128)(2,1)S(1)}, bf16[2,2,4,2,128,128]{5,4,3,2,1,0:T(8,128)(2,1)S(1)}, u32[]{:S(2)}, u32[]{:S(2)}) %collective-permute-start.27) | collective-permute-done | bytes 1048608 | tf_op jit(solution)/shard_map/ppermute | solution.py:27
  92.5 3.0 %collective-permute-start.1 = (bf16[2,5,256,256]{3,2,1,0:T(8,128)(2,1)}, bf16[2,5,256,256]{3,2,1,0:T(8,128)(2,1)}, u32[]{:S(2)}, u32[]{:S(2)}) collective-permute-start(bf16[2,5,256,256]{3,2,1,0:T(8,128)(2,1)} %get-tuple-element.44.refs_4_.refs_3_), channel_id=1, source_target_pairs={{0,96},{32,64},{96,0},{64,32},{16,112},{48,80},{112,16},{80,48},{1... | collective-permute-start | bytes 3932168 | tf_op jit(solution)/shard_map/ppermute | solution.py:27
  96.1 5.0 %collective-permute-done.3.refs_9_.refs_8_ = bf16[2,5,256,256]{3,2,1,0:T(8,128)(2,1)} collective-permute-done((bf16[2,5,256,256]{3,2,1,0:T(8,128)(2,1)S(1)}, bf16[2,5,256,256]{3,2,1,0:T(8,128)(2,1)}, u32[]{:S(2)}, u32[]{:S(2)}) %collective-permute-start.3) | collective-permute-done | bytes 1310752 | tf_op jit(solution)/shard_map/ppermute | solution.py:27
  101.1 1.7 collective-permute-start.5
  102.8 25.4 %collective-permute-done.6.refs_13_.refs_12_ = bf16[2,6,256,256]{3,2,1,0:T(8,128)(2,1)S(1)} collective-permute-done((bf16[2,6,256,256]{3,2,1,0:T(8,128)(2,1)S(1)}, bf16[2,6,256,256]{3,2,1,0:T(8,128)(2,1)S(1)}, u32[]{:S(2)}, u32[]{:S(2)}) %collective-permute-start.6) | collective-permute-done | bytes 1572896 | tf_op jit(solution)/shard_map/ppermute | solution.py:27
  128.2 1.7 collective-permute-start.8
  129.9 2.2 collective-permute-start.2
  133.3 3.1 %fusion = (bf16[2,4,256,256]{3,2,1,0:T(8,128)(2,1)}, bf16[2,4,256,256]{3,2,1,0:T(8,128)(2,1)}) fusion(bf16[2,16,256,256]{3,2,1,0:T(8,128)(2,1)} %refs_16_.1), kind=kLoop, calls=%fused_computation.5 | loop fusion | bytes 4194304 | tf_op jit(solution)/shard_map/slice | solution.py:305
  136.4 18.0 %collective-permute-done.7.refs_14_.refs_13_ = bf16[2,6,256,256]{3,2,1,0:T(8,128)(2,1)} collective-permute-done((bf16[2,6,256,256]{3,2,1,0:T(8,128)(2,1)S(1)}, bf16[2,6,256,256]{3,2,1,0:T(8,128)(2,1)}, u32[]{:S(2)}, u32[]{:S(2)}) %collective-permute-start.7) | collective-permute-done | bytes 1572896 | tf_op jit(solution)/shard_map/ppermute | solution.py:27
  155.7 4.0 %collective-permute-start.9 = (bf16[2,4,256,256]{3,2,1,0:T(8,128)(2,1)}, bf16[2,4,256,256]{3,2,1,0:T(8,128)(2,1)}, u32[]{:S(2)}, u32[]{:S(2)}) collective-permute-start(bf16[2,4,256,256]{3,2,1,0:T(8,128)(2,1)} %get-tuple-element.42), channel_id=1, source_target_pairs={{0,1},{1,2},{2,3},{3,4},{4,5},{5,6},{6,7},{7,8},{8,9},{9,10},{10,1... | collective-permute-start | bytes 3145736 | tf_op jit(solution)/shard_map/ppermute | solution.py:304
  161.3 1.7 collective-permute-done.2.refs_7_.refs_6_
  163.0 1.7 collective-permute-start.14
  164.8 21.1 %collective-permute-done.8.refs_15_.refs_14_ = bf16[2,6,256,256]{3,2,1,0:T(8,128)(2,1)} collective-permute-done((bf16[2,6,256,256]{3,2,1,0:T(8,128)(2,1)S(1)}, bf16[2,6,256,256]{3,2,1,0:T(8,128)(2,1)}, u32[]{:S(2)}, u32[]{:S(2)}) %collective-permute-start.8) | collective-permute-done | bytes 1572896 | tf_op jit(solution)/shard_map/ppermute | solution.py:27
  187.4 8.9 %partial_near.4 = (bf16[2,2,256,256]{3,2,1,0:T(8,128)(2,1)}, bf16[2,2,256,256]{3,2,1,0:T(8,128)(2,1)}, bf16[2,2,256,256]{3,2,1,0:T(8,128)(2,1)}) custom-call(s32[256]{0:T(256)} %copy-done.18, s32[256]{0:T(256)} %copy-done.17, s32[256]{0:T(256)} %copy-done.16, s32[12]{0:T(128)} %stack.69.shard_ref, ...), custom_call_target="tpu_custom_call" | custom-call | flops 3240000000 | bytes 11400000 | tf_op jit(solution)/shard_map/partial_near/pallas_call | solution.py:96
  196.4 2.3 collective-permute-start.16
  198.6 8.8 %partial_near.5 = (bf16[2,2,256,256]{3,2,1,0:T(8,128)(2,1)}, bf16[2,2,256,256]{3,2,1,0:T(8,128)(2,1)}, bf16[2,2,256,256]{3,2,1,0:T(8,128)(2,1)}) custom-call(s32[256]{0:T(256)} %copy-done.18, s32[256]{0:T(256)} %copy-done.17, s32[256]{0:T(256)} %copy-done.16, s32[12]{0:T(128)} %stack.69.shard_ref, ...), custom_call_target="tpu_custom_call" | custom-call | flops 3240000000 | bytes 11400000 | tf_op jit(solution)/shard_map/partial_near/pallas_call | solution.py:96
  211.2 18.3 %couple.1.refs_17_ = bf16[2,16,256,256]{3,2,1,0:T(8,128)(2,1)} custom-call(f32[256,288]{1,0:T(8,128)} %bitcast.20, bf16[2,4,256,256]{3,2,1,0:T(8,128)(2,1)} %collective-permute-done.9.low_ref, bf16[2,16,256,256]{3,2,1,0:T(8,128)(2,1)} %refs_16_.1, bf16[2,4,256,256]{3,2,1,0:T(8,128)(2,1)} %collective-permute-done.10.high_ref), custom_call_target="tpu_custom_call" | custom-call | flops 20000000000 | bytes 10000000 | tf_op jit(solution)/shard_map/couple/pallas_call | solution.py:268
  230.5 6.9 %partial_near.3 = (bf16[2,1,256,256]{3,2,1,0:T(8,128)(2,1)}, bf16[2,1,256,256]{3,2,1,0:T(8,128)(2,1)}, bf16[2,2,256,256]{3,2,1,0:T(8,128)(2,1)}) custom-call(s32[256]{0:T(256)} %copy-done.18, s32[256]{0:T(256)} %copy-done.17, s32[256]{0:T(256)} %copy-done.16, s32[12]{0:T(128)} %stack.69.shard_ref, bf16[1,2,4,2,128,128]{5,4,3,2,1,0:T(8,128)(2,1)} %copy-done.10, ...), custom_call_target="tpu_custom_call" | custom-call | flops 2160000000 | bytes 7600000 | tf_op jit(solution)/shard_map/partial_near/pallas_call | solution.py:96
  240.0 2.2 collective-permute-start.19
  243.5 21.4 %own_near.1.base_ref = f32[2,16,256,256]{3,2,1,0:T(8,128)} custom-call(s32[256]{0:T(256)} %copy-done.20, s32[12]{0:T(128)} %stack.69.shard_ref, bf16[16,2,8,2,128,128]{5,4,3,2,1,0:T(8,128)(2,1)} %k3.1, bf16[16,2,8,2,128,128]{5,4,3,2,1,0:T(8,128)(2,1)} %k3.1, bf16[16,2,8,2,128,128]{5,4,3,2,1,0:T(8,128)(2,1)} %k3.1, bf16[16,2,8,2,128,128]{5,4,3,2,1,0:T(8,128)(2,1)} %k3.1, ...), custom_call_target="tpu_custom_call" | custom-call | flops 8640000000 | bytes 41600000 | tf_op jit(solution)/shard_map/own_near/pallas_call | solution.py:146
  265.0 5.3 %final_sum.3.refs_0_ = bf16[2,16,256,256]{3,2,1,0:T(8,128)(2,1)} custom-call(f32[2,16,256,256]{3,2,1,0:T(8,128)} %own_near.1.base_ref, bf16[2,2,256,256]{3,2,1,0:T(8,128)(2,1)} %copy-done.6, bf16[2,2,256,256]{3,2,1,0:T(8,128)(2,1)} %copy-done.7, bf16[2,2,256,256]{3,2,1,0:T(8,128)(2,1)} %copy-done.8), custom_call_target="tpu_custom_call" | custom-call | flops 1572864 | bytes 6300000 | tf_op jit(solution)/shard_map/final_sum/pallas_call | solution.py:176
  271.1 5.2 %final_sum.4.refs_0_ = bf16[2,16,256,256]{3,2,1,0:T(8,128)(2,1)} custom-call(f32[2,16,256,256]{3,2,1,0:T(8,128)} %own_near.1.base_ref, bf16[2,2,256,256]{3,2,1,0:T(8,128)(2,1)} %copy-done.9, bf16[2,2,256,256]{3,2,1,0:T(8,128)(2,1)} %copy-done.13, bf16[2,2,256,256]{3,2,1,0:T(8,128)(2,1)} %collective-permute-done.25.o2, ...), custom_call_target="tpu_custom_call", output_to_operand_aliasing={{}: (4, {})} | custom-call | flops 1572864 | bytes 6300000 | tf_op jit(solution)/shard_map/final_sum/pallas_call | solution.py:176
  277.9 3.9 %final_sum.5 = bf16[2,16,256,256]{3,2,1,0:T(8,128)(2,1)} custom-call(f32[2,16,256,256]{3,2,1,0:T(8,128)} %own_near.1.base_ref, bf16[2,1,256,256]{3,2,1,0:T(8,128)(2,1)} %copy-done.14, bf16[2,1,256,256]{3,2,1,0:T(8,128)(2,1)} %collective-permute-done.18.o1, bf16[2,2,256,256]{3,2,1,0:T(8,128)(2,1)} %copy-done.12, ...), custom_call_target="tpu_custom_call", output_to_operand_aliasing={{}: (4, {})} | custom-call | flops 1048576 | bytes 4200000 | tf_op jit(solution)/shard_map/final_sum/pallas_call | solution.py:176
  (102 shorter events, 25.4 us)
Async XLA Ops:
  14.7 51.4 %collective-permute-start.20 = (bf16[2,2,4,2,128,128]{5,4,3,2,1,0:T(8,128)(2,1)}, bf16[2,2,4,2,128,128]{5,4,3,2,1,0:T(8,128)(2,1)}, u32[]{:S(2)}, u32[]{:S(2)}) collective-permute-start(bf16[2,2,4,2,128,128]{5,4,3,2,1,0:T(8,128)(2,1)} %get-tuple-element.29), channel_id=1, source_target_pairs={{0,16},{32,48},{96,112},{64,80},{16,0},{48,32},{112,96},{80,64},{1... | collective-permute-start | bytes 3145736 | tf_op jit(solution)/shard_map/ppermute | solution.py:27
  16.8 49.7 %collective-permute-start.21 = (bf16[2,2,4,2,128,128]{5,4,3,2,1,0:T(8,128)(2,1)}, bf16[2,2,4,2,128,128]{5,4,3,2,1,0:T(8,128)(2,1)}, u32[]{:S(2)}, u32[]{:S(2)}) collective-permute-start(bf16[2,2,4,2,128,128]{5,4,3,2,1,0:T(8,128)(2,1)} %get-tuple-element.30), channel_id=1, source_target_pairs={{0,32},{32,0},{96,64},{64,96},{16,48},{48,16},{112,80},{80,112},{1... | collective-permute-start | bytes 3145736 | tf_op jit(solution)/shard_map/ppermute | solution.py:27
  18.4 49.7 %collective-permute-start.22 = (bf16[2,2,4,2,128,128]{5,4,3,2,1,0:T(8,128)(2,1)}, bf16[2,2,4,2,128,128]{5,4,3,2,1,0:T(8,128)(2,1)}, u32[]{:S(2)}, u32[]{:S(2)}) collective-permute-start(bf16[2,2,4,2,128,128]{5,4,3,2,1,0:T(8,128)(2,1)} %get-tuple-element.31), channel_id=1, source_target_pairs={{0,96},{32,64},{96,0},{64,32},{16,112},{48,80},{112,16},{80,48},{1... | collective-permute-start | bytes 3145736 | tf_op jit(solution)/shard_map/ppermute | solution.py:27
  20.6 49.7 %collective-permute-start.26 = (bf16[2,2,4,2,128,128]{5,4,3,2,1,0:T(8,128)(2,1)}, bf16[2,2,4,2,128,128]{5,4,3,2,1,0:T(8,128)(2,1)}, u32[]{:S(2)}, u32[]{:S(2)}) collective-permute-start(bf16[2,2,4,2,128,128]{5,4,3,2,1,0:T(8,128)(2,1)} %get-tuple-element.35), channel_id=1, source_target_pairs={{0,16},{32,48},{96,112},{64,80},{16,0},{48,32},{112,96},{80,64},{1... | collective-permute-start | bytes 3145736 | tf_op jit(solution)/shard_map/ppermute | solution.py:27
  20.9 23.4 %collective-permute-start.13 = (s32[256]{0:T(256)S(1)}, s32[256]{0:T(256)S(1)}, u32[]{:S(2)}, u32[]{:S(2)}) collective-permute-start(s32[256]{0:T(256)S(1)} %reshape.56.index_ref), channel_id=1, source_target_pairs={{0,96},{32,64},{96,0},{64,32},{16,112},{48,80},{112,16},{80,48},{1... | collective-permute-start | bytes 3080 | tf_op jit(solution)/shard_map/ppermute | solution.py:27
  44.3 3.6 %collective-permute-start.12 = (s32[256]{0:T(256)S(1)}, s32[256]{0:T(256)S(1)}, u32[]{:S(2)}, u32[]{:S(2)}) collective-permute-start(s32[256]{0:T(256)S(1)} %reshape.56.index_ref), channel_id=1, source_target_pairs={{0,32},{32,0},{96,64},{64,96},{16,48},{48,16},{112,80},{80,112},{1... | collective-permute-start | bytes 3080 | tf_op jit(solution)/shard_map/ppermute | solution.py:27
  47.8 14.9 %collective-permute-start.11 = (s32[256]{0:T(256)S(1)}, s32[256]{0:T(256)S(1)}, u32[]{:S(2)}, u32[]{:S(2)}) collective-permute-start(s32[256]{0:T(256)S(1)} %reshape.56.index_ref), channel_id=1, source_target_pairs={{0,16},{32,48},{96,112},{64,80},{16,0},{48,32},{112,96},{80,64},{1... | collective-permute-start | bytes 3080 | tf_op jit(solution)/shard_map/ppermute | solution.py:27
  62.8 32.8 %collective-permute-start.4 = (bf16[2,5,256,256]{3,2,1,0:T(8,128)(2,1)S(1)}, bf16[2,5,256,256]{3,2,1,0:T(8,128)(2,1)S(1)}, u32[]{:S(2)}, u32[]{:S(2)}) collective-permute-start(bf16[2,5,256,256]{3,2,1,0:T(8,128)(2,1)S(1)} %get-tuple-element.43.refs_8_.refs_7_), channel_id=1, source_target_pairs={{0,16},{32,48},{96,112},{64,80},{16,0},{48,32},{112,96},{80,64},{1... | collective-permute-start | bytes 3932168 | tf_op jit(solution)/shard_map/ppermute | solution.py:27
  66.1 62.1 %collective-permute-start.6 = (bf16[2,6,256,256]{3,2,1,0:T(8,128)(2,1)S(1)}, bf16[2,6,256,256]{3,2,1,0:T(8,128)(2,1)S(1)}, u32[]{:S(2)}, u32[]{:S(2)}) collective-permute-start(bf16[2,6,256,256]{3,2,1,0:T(8,128)(2,1)S(1)} %slice.17.refs_12_.refs_11_), channel_id=1, source_target_pairs={{0,16},{32,48},{96,112},{64,80},{16,0},{48,32},{112,96},{80,64},{1... | collective-permute-start | bytes 4718600 | tf_op jit(solution)/shard_map/ppermute | solution.py:27
  66.5 26.0 %collective-permute-start.27 = (bf16[2,2,4,2,128,128]{5,4,3,2,1,0:T(8,128)(2,1)S(1)}, bf16[2,2,4,2,128,128]{5,4,3,2,1,0:T(8,128)(2,1)S(1)}, u32[]{:S(2)}, u32[]{:S(2)}) collective-permute-start(bf16[2,2,4,2,128,128]{5,4,3,2,1,0:T(8,128)(2,1)S(1)} %copy-done.22), channel_id=1, source_target_pairs={{0,32},{32,0},{96,64},{64,96},{16,48},{48,16},{112,80},{80,112},{1... | collective-permute-start | bytes 3145736 | tf_op jit(solution)/shard_map/ppermute | solution.py:27
  68.1 33.0 %collective-permute-start.3 = (bf16[2,5,256,256]{3,2,1,0:T(8,128)(2,1)S(1)}, bf16[2,5,256,256]{3,2,1,0:T(8,128)(2,1)}, u32[]{:S(2)}, u32[]{:S(2)}) collective-permute-start(bf16[2,5,256,256]{3,2,1,0:T(8,128)(2,1)S(1)} %get-tuple-element.43.refs_8_.refs_7_), channel_id=1, source_target_pairs={{0,96},{32,64},{96,0},{64,32},{16,112},{48,80},{112,16},{80,48},{1... | collective-permute-start | bytes 3932168 | tf_op jit(solution)/shard_map/ppermute | solution.py:27
  70.3 59.6 %collective-permute-start = (bf16[2,5,256,256]{3,2,1,0:T(8,128)(2,1)}, bf16[2,5,256,256]{3,2,1,0:T(8,128)(2,1)}, u32[]{:S(2)}, u32[]{:S(2)}) collective-permute-start(bf16[2,5,256,256]{3,2,1,0:T(8,128)(2,1)} %get-tuple-element.44.refs_4_.refs_3_), channel_id=1, source_target_pairs={{0,32},{32,0},{96,64},{64,96},{16,48},{48,16},{112,80},{80,112},{1... | collective-permute-start | bytes 3932168 | tf_op jit(solution)/shard_map/ppermute | solution.py:27
  92.5 39.6 %collective-permute-start.1 = (bf16[2,5,256,256]{3,2,1,0:T(8,128)(2,1)}, bf16[2,5,256,256]{3,2,1,0:T(8,128)(2,1)}, u32[]{:S(2)}, u32[]{:S(2)}) collective-permute-start(bf16[2,5,256,256]{3,2,1,0:T(8,128)(2,1)} %get-tuple-element.44.refs_4_.refs_3_), channel_id=1, source_target_pairs={{0,96},{32,64},{96,0},{64,32},{16,112},{48,80},{112,16},{80,48},{1... | collective-permute-start | bytes 3932168 | tf_op jit(solution)/shard_map/ppermute | solution.py:27
  95.6 58.9 %collective-permute-start.7 = (bf16[2,6,256,256]{3,2,1,0:T(8,128)(2,1)S(1)}, bf16[2,6,256,256]{3,2,1,0:T(8,128)(2,1)}, u32[]{:S(2)}, u32[]{:S(2)}) collective-permute-start(bf16[2,6,256,256]{3,2,1,0:T(8,128)(2,1)S(1)} %slice.17.refs_12_.refs_11_), channel_id=1, source_target_pairs={{0,32},{32,0},{96,64},{64,96},{16,48},{48,16},{112,80},{80,112},{1... | collective-permute-start | bytes 4718600 | tf_op jit(solution)/shard_map/ppermute | solution.py:27
  101.1 54.7 %collective-permute-start.5 = (bf16[2,5,256,256]{3,2,1,0:T(8,128)(2,1)}, bf16[2,5,256,256]{3,2,1,0:T(8,128)(2,1)}, u32[]{:S(2)}, u32[]{:S(2)}) collective-permute-start(bf16[2,5,256,256]{3,2,1,0:T(8,128)(2,1)} %collective-permute-done.3.refs_9_.refs_8_), channel_id=1, source_target_pairs={{0,16},{32,48},{96,112},{64,80},{16,0},{48,32},{112,96},{80,64},{1... | collective-permute-start | bytes 3932168 | tf_op jit(solution)/shard_map/ppermute | solution.py:27
  128.2 57.7 %collective-permute-start.8 = (bf16[2,6,256,256]{3,2,1,0:T(8,128)(2,1)S(1)}, bf16[2,6,256,256]{3,2,1,0:T(8,128)(2,1)}, u32[]{:S(2)}, u32[]{:S(2)}) collective-permute-start(bf16[2,6,256,256]{3,2,1,0:T(8,128)(2,1)S(1)} %collective-permute-done.6.refs_13_.refs_12_), channel_id=1, source_target_pairs={{0,32},{32,0},{96,64},{64,96},{16,48},{48,16},{112,80},{80,112},{1... | collective-permute-start | bytes 4718600 | tf_op jit(solution)/shard_map/ppermute | solution.py:27
  129.9 33.2 %collective-permute-start.2 = (bf16[2,5,256,256]{3,2,1,0:T(8,128)(2,1)}, bf16[2,5,256,256]{3,2,1,0:T(8,128)(2,1)}, u32[]{:S(2)}, u32[]{:S(2)}) collective-permute-start(bf16[2,5,256,256]{3,2,1,0:T(8,128)(2,1)} %collective-permute-done.refs_5_.refs_4_), channel_id=1, source_target_pairs={{0,96},{32,64},{96,0},{64,32},{16,112},{48,80},{112,16},{80,48},{1... | collective-permute-start | bytes 3932168 | tf_op jit(solution)/shard_map/ppermute | solution.py:27
  132.2 64.2 %collective-permute-start.28 = (bf16[2,2,4,2,128,128]{5,4,3,2,1,0:T(8,128)(2,1)}, bf16[2,2,4,2,128,128]{5,4,3,2,1,0:T(8,128)(2,1)}, u32[]{:S(2)}, u32[]{:S(2)}) collective-permute-start(bf16[2,2,4,2,128,128]{5,4,3,2,1,0:T(8,128)(2,1)} %get-tuple-element.37), channel_id=1, source_target_pairs={{0,96},{32,64},{96,0},{64,32},{16,112},{48,80},{112,16},{80,48},{1... | collective-permute-start | bytes 3145736 | tf_op jit(solution)/shard_map/ppermute | solution.py:27
  154.4 55.4 %collective-permute-start.10 = (bf16[2,4,256,256]{3,2,1,0:T(8,128)(2,1)}, bf16[2,4,256,256]{3,2,1,0:T(8,128)(2,1)}, u32[]{:S(2)}, u32[]{:S(2)}) collective-permute-start(bf16[2,4,256,256]{3,2,1,0:T(8,128)(2,1)} %get-tuple-element.41), channel_id=1, source_target_pairs={{1,0},{2,1},{3,2},{4,3},{5,4},{6,5},{7,6},{8,7},{9,8},{10,9},{11,1... | collective-permute-start | bytes 3145736 | tf_op jit(solution)/shard_map/ppermute | solution.py:305
  155.7 54.8 %collective-permute-start.9 = (bf16[2,4,256,256]{3,2,1,0:T(8,128)(2,1)}, bf16[2,4,256,256]{3,2,1,0:T(8,128)(2,1)}, u32[]{:S(2)}, u32[]{:S(2)}) collective-permute-start(bf16[2,4,256,256]{3,2,1,0:T(8,128)(2,1)} %get-tuple-element.42), channel_id=1, source_target_pairs={{0,1},{1,2},{2,3},{3,4},{4,5},{5,6},{6,7},{7,8},{8,9},{9,10},{10,1... | collective-permute-start | bytes 3145736 | tf_op jit(solution)/shard_map/ppermute | solution.py:304
  163.0 44.4 %collective-permute-start.14 = (bf16[1,2,4,2,128,128]{5,4,3,2,1,0:T(8,128)(2,1)}, bf16[1,2,4,2,128,128]{5,4,3,2,1,0:T(8,128)(2,1)S(1)}, u32[]{:S(2)}, u32[]{:S(2)}) collective-permute-start(bf16[1,2,4,2,128,128]{5,4,3,2,1,0:T(8,128)(2,1)} %get-tuple-element.23), channel_id=1, source_target_pairs={{0,16},{32,48},{96,112},{64,80},{16,0},{48,32},{112,96},{80,64},{1... | collective-permute-start | bytes 1572872 | tf_op jit(solution)/shard_map/ppermute | solution.py:27
  185.9 23.2 %collective-permute-start.15 = (bf16[1,2,4,2,128,128]{5,4,3,2,1,0:T(8,128)(2,1)}, bf16[1,2,4,2,128,128]{5,4,3,2,1,0:T(8,128)(2,1)S(1)}, u32[]{:S(2)}, u32[]{:S(2)}) collective-permute-start(bf16[1,2,4,2,128,128]{5,4,3,2,1,0:T(8,128)(2,1)} %get-tuple-element.24), channel_id=1, source_target_pairs={{0,32},{32,0},{96,64},{64,96},{16,48},{48,16},{112,80},{80,112},{1... | collective-permute-start | bytes 1572872 | tf_op jit(solution)/shard_map/ppermute | solution.py:27
  196.4 33.1 %collective-permute-start.16 = (bf16[2,2,4,2,128,128]{5,4,3,2,1,0:T(8,128)(2,1)}, bf16[2,2,4,2,128,128]{5,4,3,2,1,0:T(8,128)(2,1)S(1)}, u32[]{:S(2)}, u32[]{:S(2)}) collective-permute-start(bf16[2,2,4,2,128,128]{5,4,3,2,1,0:T(8,128)(2,1)} %get-tuple-element.25), channel_id=1, source_target_pairs={{0,96},{32,64},{96,0},{64,32},{16,112},{48,80},{112,16},{80,48},{1... | collective-permute-start | bytes 3145736 | tf_op jit(solution)/shard_map/ppermute | solution.py:27
  207.5 31.3 %collective-permute-start.23 = (bf16[2,2,256,256]{3,2,1,0:T(8,128)(2,1)}, bf16[2,2,256,256]{3,2,1,0:T(8,128)(2,1)S(1)}, u32[]{:S(2)}, u32[]{:S(2)}) collective-permute-start(bf16[2,2,256,256]{3,2,1,0:T(8,128)(2,1)} %get-tuple-element.32), channel_id=1, source_target_pairs={{0,16},{32,48},{96,112},{64,80},{16,0},{48,32},{112,96},{80,64},{1... | collective-permute-start | bytes 1572872 | tf_op jit(solution)/shard_map/ppermute | solution.py:27
  209.1 30.9 %collective-permute-start.29 = (bf16[2,2,256,256]{3,2,1,0:T(8,128)(2,1)}, bf16[2,2,256,256]{3,2,1,0:T(8,128)(2,1)S(1)}, u32[]{:S(2)}, u32[]{:S(2)}) collective-permute-start(bf16[2,2,256,256]{3,2,1,0:T(8,128)(2,1)} %get-tuple-element.38), channel_id=1, source_target_pairs={{0,16},{32,48},{96,112},{64,80},{16,0},{48,32},{112,96},{80,64},{1... | collective-permute-start | bytes 1572872 | tf_op jit(solution)/shard_map/ppermute | solution.py:27
  209.9 32.2 %collective-permute-start.30 = (bf16[2,2,256,256]{3,2,1,0:T(8,128)(2,1)}, bf16[2,2,256,256]{3,2,1,0:T(8,128)(2,1)S(1)}, u32[]{:S(2)}, u32[]{:S(2)}) collective-permute-start(bf16[2,2,256,256]{3,2,1,0:T(8,128)(2,1)} %get-tuple-element.39), channel_id=1, source_target_pairs={{0,32},{32,0},{96,64},{64,96},{16,48},{48,16},{112,80},{80,112},{1... | collective-permute-start | bytes 1572872 | tf_op jit(solution)/shard_map/ppermute | solution.py:27
  210.6 32.3 %collective-permute-start.31 = (bf16[2,2,256,256]{3,2,1,0:T(8,128)(2,1)}, bf16[2,2,256,256]{3,2,1,0:T(8,128)(2,1)S(1)}, u32[]{:S(2)}, u32[]{:S(2)}) collective-permute-start(bf16[2,2,256,256]{3,2,1,0:T(8,128)(2,1)} %get-tuple-element.40), channel_id=1, source_target_pairs={{0,96},{32,64},{96,0},{64,32},{16,112},{48,80},{112,16},{80,48},{1... | collective-permute-start | bytes 1572872 | tf_op jit(solution)/shard_map/ppermute | solution.py:27
  237.4 39.0 %collective-permute-start.17 = (bf16[2,1,256,256]{3,2,1,0:T(8,128)(2,1)}, bf16[2,1,256,256]{3,2,1,0:T(8,128)(2,1)S(1)}, u32[]{:S(2)}, u32[]{:S(2)}) collective-permute-start(bf16[2,1,256,256]{3,2,1,0:T(8,128)(2,1)} %get-tuple-element.26), channel_id=1, source_target_pairs={{0,16},{32,48},{96,112},{64,80},{16,0},{48,32},{112,96},{80,64},{1... | collective-permute-start | bytes 786440 | tf_op jit(solution)/shard_map/ppermute | solution.py:27
  238.8 37.6 %collective-permute-start.18 = (bf16[2,1,256,256]{3,2,1,0:T(8,128)(2,1)}, bf16[2,1,256,256]{3,2,1,0:T(8,128)(2,1)}, u32[]{:S(2)}, u32[]{:S(2)}) collective-permute-start(bf16[2,1,256,256]{3,2,1,0:T(8,128)(2,1)} %get-tuple-element.27), channel_id=1, source_target_pairs={{0,32},{32,0},{96,64},{64,96},{16,48},{48,16},{112,80},{80,112},{1... | collective-permute-start | bytes 786440 | tf_op jit(solution)/shard_map/ppermute | solution.py:27
  240.0 36.4 %collective-permute-start.19 = (bf16[2,2,256,256]{3,2,1,0:T(8,128)(2,1)}, bf16[2,2,256,256]{3,2,1,0:T(8,128)(2,1)S(1)}, u32[]{:S(2)}, u32[]{:S(2)}) collective-permute-start(bf16[2,2,256,256]{3,2,1,0:T(8,128)(2,1)} %get-tuple-element.28), channel_id=1, source_target_pairs={{0,96},{32,64},{96,0},{64,32},{16,112},{48,80},{112,16},{80,48},{1... | collective-permute-start | bytes 1572872 | tf_op jit(solution)/shard_map/ppermute | solution.py:27
  242.1 28.2 %collective-permute-start.24 = (bf16[2,2,256,256]{3,2,1,0:T(8,128)(2,1)}, bf16[2,2,256,256]{3,2,1,0:T(8,128)(2,1)S(1)}, u32[]{:S(2)}, u32[]{:S(2)}) collective-permute-start(bf16[2,2,256,256]{3,2,1,0:T(8,128)(2,1)} %get-tuple-element.33), channel_id=1, source_target_pairs={{0,32},{32,0},{96,64},{64,96},{16,48},{48,16},{112,80},{80,112},{1... | collective-permute-start | bytes 1572872 | tf_op jit(solution)/shard_map/ppermute | solution.py:27
  242.8 27.5 %collective-permute-start.25 = (bf16[2,2,256,256]{3,2,1,0:T(8,128)(2,1)}, bf16[2,2,256,256]{3,2,1,0:T(8,128)(2,1)}, u32[]{:S(2)}, u32[]{:S(2)}) collective-permute-start(bf16[2,2,256,256]{3,2,1,0:T(8,128)(2,1)} %get-tuple-element.34), channel_id=1, source_target_pairs={{0,96},{32,64},{96,0},{64,32},{16,112},{48,80},{112,16},{80,48},{1... | collective-permute-start | bytes 1572872 | tf_op jit(solution)/shard_map/ppermute | solution.py:27
  (24 other events, 499.7 us)
